TPU v7x, 256 devices: a whole 4x4x8 slice. The times are simulated.
256 devices in a mesh: ctx: 128 (over z, x, y_hi, core), head: 2 (over y_lo).
Axes of the slice: x: 4, y: 4 (y_hi: 2, y_lo: 2; y = y_hi * 2 + y_lo), z: 8, core: 2. Of those that a mesh axis runs over, the one named last changes fastest.
Arguments:
- fw_q: bfloat16 [32768, 2048], P('ctx', 'head'), may hold values from -6 to 6
- fw_k: bfloat16 [32768, 2048], P('ctx', 'head'), may hold values from -16 to 16
- fw_v: bfloat16 [32768, 2048], P('ctx', 'head'), may hold values from -6 to 6
- fw_lr: float32 [32768, 4], P('ctx', 'head'), may hold values from 0.1 to 3
- fast_gate: bfloat16 [4, 512, 512], P('head'), may hold values from -0.25 to 0.25
- fast_up: bfloat16 [4, 512, 512], P('head'), may hold values from -0.25 to 0.25
- fast_down: bfloat16 [4, 512, 512], P('head'), may hold values from -0.25 to 0.25
- attn_q: bfloat16 [32768, 2048], P('ctx', 'head'), may hold values from -96 to 96
- attn_k: bfloat16 [32768, 2048], P('ctx', 'head'), may hold values from -10 to 10
- attn_v: bfloat16 [32768, 2048], P('ctx', 'head'), may hold values from -6 to 6
Outputs:
- mixed_out: bfloat16 [32768, 2048], P(('ctx', 'head'))
All inputs are finite; a program needn't handle non-finite values.
Results may differ from a plain program's by a relative error of at most 0.0095.
Values may be sent and summed in bfloat16 or wider, within the bound.
No kernel may reach another device: no remote copies, remote signals or barrier semaphores. Data moves between devices by JAX's collectives and lax.ppermute only.
A program may use at most 128 MiB of HBM per device.

v0:
```python
import math

import jax
import jax.numpy as jnp
from jax import lax
from jax.sharding import PartitionSpec as P

SWA_DH = 128
WINDOW = 128
NS_ITERS = 2


linear_coef = 3.4445
square_coef = -4.775
quartic_coef = 2.0315
epsilon = 1e-06


def passed_along(value, axis, steps):
    count = lax.axis_size(axis)
    first, last = (max(0, -steps), min(count, count - steps))
    return lax.ppermute(value, axis, [(source, source + steps) for source in range(first, last)])


def refresh(weight, update):
    initial = weight.astype(jnp.float32)
    stepped = initial - update.astype(jnp.float32)
    old_norm = jnp.sqrt(jnp.sum(initial * initial, axis=-2, keepdims=True) + epsilon)
    new_norm = jnp.sqrt(jnp.sum(stepped * stepped, axis=-2, keepdims=True) + epsilon)
    return (stepped * (old_norm / new_norm)).astype(jnp.bfloat16)


def attend(query_rows, key_window, value_window, device_index):
    row_count = query_rows.shape[0]
    key_count = key_window.shape[0]
    head_total = query_rows.shape[1] // SWA_DH
    query_heads = query_rows.reshape(row_count, head_total, SWA_DH)
    key_heads = key_window.reshape(key_count, head_total, SWA_DH)
    value_heads = value_window.reshape(key_count, head_total, SWA_DH)
    score_scale = 1.0 / math.sqrt(SWA_DH)
    scores = (
        jnp.einsum("qhd,khd->hqk", query_heads, key_heads, preferred_element_type=jnp.float32)
        * score_scale
    )
    query_pos = device_index * row_count + jnp.arange(row_count, dtype=jnp.int32)
    key_pos = device_index * row_count - WINDOW + jnp.arange(key_count, dtype=jnp.int32)
    allowed = (
        (key_pos[None, :] <= query_pos[:, None])
        & (key_pos[None, :] > query_pos[:, None] - WINDOW)
        & (key_pos[None, :] >= 0)
    )
    masked = jnp.where(allowed[None, :, :], scores, -jnp.inf)
    row_peak = jnp.max(masked, axis=-1, keepdims=True)
    exponent = jnp.exp(masked - row_peak)
    row_total = jnp.sum(exponent, axis=-1, keepdims=True)
    weights_bf = (exponent / row_total).astype(jnp.bfloat16)
    result = jnp.einsum("hqk,khd->qhd", weights_bf, value_heads, preferred_element_type=jnp.float32)
    return result.reshape(row_count, head_total * SWA_DH)


def shards(fw_q, fw_k, fw_v, fw_lr, fast_gate, fast_up, fast_down, attn_q, attn_k, attn_v):
    tokens_here = fw_k.shape[0]
    head_count = fast_gate.shape[0]
    head_width = fast_gate.shape[1]
    groups = lax.axis_size("head")
    device_index = lax.axis_index("ctx") * groups + lax.axis_index("head")
    moved_q, moved_k, moved_v = (
        lax.all_to_all(attn_q, "head", split_axis=0, concat_axis=1, tiled=True),
        lax.all_to_all(attn_k, "head", split_axis=0, concat_axis=1, tiled=True),
        lax.all_to_all(attn_v, "head", split_axis=0, concat_axis=1, tiled=True),
    )
    previous = passed_along(jnp.stack([moved_k, moved_v]), ("ctx", "head"), 1)
    key_window = jnp.concatenate([previous[0], moved_k], axis=0)
    value_window = jnp.concatenate([previous[1], moved_v], axis=0)
    key_heads = fw_k.reshape(tokens_here, head_count, head_width)
    value_heads = fw_v.reshape(tokens_here, head_count, head_width)
    query_heads = fw_q.reshape(tokens_here, head_count, head_width)
    pre_gate = jnp.einsum("thi,hij->thj", key_heads, fast_gate, preferred_element_type=jnp.float32)
    pre_up = jnp.einsum("thi,hij->thj", key_heads, fast_up, preferred_element_type=jnp.float32)
    sigmoid_gate = jax.nn.sigmoid(pre_gate)
    activated = pre_gate * sigmoid_gate
    hidden = (activated * pre_up).astype(jnp.bfloat16)
    out_grad = (-(fw_lr[:, :, None] * value_heads.astype(jnp.float32))).astype(jnp.bfloat16)
    grad_down = jnp.einsum("thi,thj->hij", hidden, out_grad, preferred_element_type=jnp.float32)
    hidden_grad = jnp.einsum(
        "thj,hij->thi", out_grad, fast_down, preferred_element_type=jnp.float32
    )
    slope = sigmoid_gate * (1.0 + pre_gate * (1.0 - sigmoid_gate))
    gate_grad = (hidden_grad * pre_up * slope).astype(jnp.bfloat16)
    up_grad = (hidden_grad * activated).astype(jnp.bfloat16)
    grad_gate = jnp.einsum("thi,thj->hij", key_heads, gate_grad, preferred_element_type=jnp.float32)
    grad_up = jnp.einsum("thi,thj->hij", key_heads, up_grad, preferred_element_type=jnp.float32)
    gradients = jnp.stack([grad_gate, grad_up, grad_down], axis=1)
    summed = lax.psum(gradients, "ctx")
    norm_total = jnp.sum(summed * summed, axis=(2, 3))
    iterate = (summed / jnp.sqrt(norm_total + epsilon)[:, :, None, None]).astype(jnp.bfloat16)
    for sweep_index in range(NS_ITERS):
        gram_matrix = jnp.einsum(
            "abij,abkj->abik", iterate, iterate, preferred_element_type=jnp.float32
        ).astype(jnp.bfloat16)
        square = jnp.einsum(
            "abij,abjk->abik", gram_matrix, gram_matrix, preferred_element_type=jnp.float32
        )
        polynomial = (square_coef * gram_matrix.astype(jnp.float32) + quartic_coef * square).astype(
            jnp.bfloat16
        )
        iterate = (
            linear_coef * iterate.astype(jnp.float32)
            + jnp.einsum("abij,abjk->abik", polynomial, iterate, preferred_element_type=jnp.float32)
        ).astype(jnp.bfloat16)
    renewed = refresh(jnp.stack([fast_gate, fast_up, fast_down], axis=1), iterate)
    query_gate = jnp.einsum(
        "thi,hij->thj", query_heads, renewed[:, 0], preferred_element_type=jnp.float32
    )
    query_up = jnp.einsum(
        "thi,hij->thj", query_heads, renewed[:, 1], preferred_element_type=jnp.float32
    )
    query_hidden = (jax.nn.silu(query_gate) * query_up).astype(jnp.bfloat16)
    memory = jnp.einsum(
        "thi,hij->thj", query_hidden, renewed[:, 2], preferred_element_type=jnp.float32
    ).astype(jnp.bfloat16)
    memory = memory.reshape(tokens_here, head_count * head_width)
    memory_rows = lax.all_to_all(memory, "head", split_axis=0, concat_axis=1, tiled=True)
    attended = attend(moved_q, key_window, value_window, device_index)
    return (memory_rows.astype(jnp.float32) + attended).astype(jnp.bfloat16)


def solution(mesh):
    in_specs = (
        P("ctx", "head"),
        P("ctx", "head"),
        P("ctx", "head"),
        P("ctx", "head"),
        P("head", None, None),
        P("head", None, None),
        P("head", None, None),
        P("ctx", "head"),
        P("ctx", "head"),
        P("ctx", "head"),
    )
    out_specs = P(("ctx", "head"), None)
    return jax.shard_map(shards, mesh=mesh, in_specs=in_specs, out_specs=out_specs, check_vma=False)
```

profile of v0, /device:TPU:4, one launch (start us, length us, event | category | flops | bytes accessed | tf_op | source)
XLA Modules:
  0.0 1341.3 jit_solution(12975118643675689493)
XLA Ops:
  6.5 2.0 convolution_bitcast_fusion.3
  8.5 1.5 convolution_bitcast_fusion.4
  10.1 0.5 convolution_bitcast_fusion.7
  10.7 0.7 convolution_bitcast_fusion
  11.4 0.3 copy-done.7
  11.7 0.7 convolution_bitcast_fusion.2
  12.4 0.6 convolution_bitcast_fusion.1
  12.9 3.4 pad_maximum_fusion
  16.3 3.6 all-to-all-start.1
  20.0 1.0 copy.180
  21.0 7.2 all-to-all-done.1
  28.2 3.5 all-to-all-start.2
  31.7 0.3 copy.179
  32.0 8.1 all-to-all-done.2
  40.1 1.2 pad_maximum_fusion.2
  41.3 2.2 collective-permute-start
  43.5 3.5 all-to-all-start.3
  47.1 0.5 copy.150
  47.7 1.9 copy.151
  49.6 2.7 copy.152
  52.2 0.1 and_and_fusion
  52.4 1.0 copy.183
  53.4 21.4 %all-to-all-done.3 = bf16[2,128,1024]{2,1,0:T(8,128)(2,1)S(1)} async-done(((bf16[2,128,1024]{2,1,0:T(8,128)(2,1)}), bf16[2,128,1024]{2,1,0:T(8,128)(2,1)S(1)}, u32[]{:S(2)}, u32[]{:S(2)}) %all-to-all-start.3) | async-done | bytes 524320 | tf_op jit(solution)/shard_map/all_to_all | solution.py:68
  74.8 1.0 copy.184
  75.8 2.1 fusion.75
  77.9 1.0 copy.182
  78.9 3.3 fusion.76
  82.2 1211.7 %all-reduce.2.cloned.1.call-done = f32[2,3,512,512]{2,3,0,1:T(8,128)} async-done(((f32[2,3,512,512]{2,3,0,1:T(8,128)}), f32[2,3,512,512]{2,3,0,1:T(8,128)}) %all-reduce.2.cloned.1.call-update) | async-done | bytes 6291472 | tf_op jit(solution)/shard_map/psum | solution.py:94
  1293.9 3.7 multiply_reduce_fusion.1
  1297.6 0.9 copy-done
  1298.5 1.0 divide_convert_fusion
  1299.5 1.8 fusion.4
  1301.4 1.9 add_convert_fusion.3
  1303.3 1.8 add_convert_fusion.2
  1305.1 1.8 fusion.2
  1307.0 1.9 add_convert_fusion.1
  1309.0 2.9 fusion.1
  1312.0 2.3 multiply_convert_fusion
  1314.3 1.5 convolution_bitcast_fusion.6
  1315.8 3.1 fusion.19
  1318.9 1.3 all_to_all.46
  1320.1 0.9 copy.178
  1321.0 3.5 all-to-all-start
  1324.5 2.0 fusion.22
  1326.6 0.3 copy.188
  1326.9 6.2 all-to-all-done
  1333.2 0.3 copy.187
  1333.5 0.9 add_convert_fusion.4
  (40 shorter events, 0.3 us)
Async XLA Ops:
  6.5 2.0 copy-start.5
  6.5 3.5 copy-start.10
  6.5 1287.4 %all-reduce.2.cloned.1.call-start = ((), (), s32[]{:S(2)}) async-start(), calls=%async_computation.4 | async-start | bytes 12582912 | tf_op jit(solution)/shard_map/psum | solution.py:94
  6.5 3.6 copy-start.6
  6.5 3.6 copy-start.15
  10.6 1.0 copy-start.7
  16.3 3.7 copy-start.12
  16.3 11.9 all-to-all-start.1
  20.0 27.1 %copy-start.4 = (bf16[2,512,512]{2,1,0:T(8,128)(2,1)S(1)}, bf16[2,512,512]{2,1,0:T(8,128)(2,1)}, u32[]{:S(2)}) copy-start(bf16[2,512,512]{2,1,0:T(8,128)(2,1)} %param.14) | copy-start | bytes 3145732
  28.2 11.9 all-to-all-start.2
  40.1 7.0 copy-start.8
  41.3 34.4 %collective-permute-start = (bf16[2,128,2048]{1,2,0:T(8,128)(2,1)}, bf16[2,128,2048]{1,2,0:T(8,128)(2,1)}, u32[]{:S(2)}, u32[]{:S(2)}) collective-permute-start(bf16[2,128,2048]{1,2,0:T(8,128)(2,1)} %pad_maximum_fusion.2), channel_id=1, source_target_pairs={{0,1},{1,2},{2,3},{3,4},{4,5},{5,6},{6,7},{7,8},{8,9},{9,10},{10,1... | collective-permute-start | bytes 3145736 | tf_op jit(solution)/shard_map/ppermute | solution.py:22
  43.5 31.2 %all-to-all-start.3 = ((bf16[2,128,1024]{2,1,0:T(8,128)(2,1)}), bf16[2,128,1024]{2,1,0:T(8,128)(2,1)S(1)}, u32[]{:S(2)}, u32[]{:S(2)}) async-start(bf16[2,128,1024]{2,1,0:T(8,128)(2,1)} %bitcast.131), calls=%async_computation.3 | async-start | bytes 1048576 | tf_op jit(solution)/shard_map/all_to_all | solution.py:68
  47.7 1261.3 %copy-start.1 = (bf16[2,512,512]{1,2,0:T(8,128)(2,1)}, bf16[2,512,512]{1,2,0:T(8,128)(2,1)S(1)}, u32[]{:S(2)}) copy-start(bf16[2,512,512]{1,2,0:T(8,128)(2,1)S(1)} %copy.150) | copy-start | bytes 3145732
  49.6 1259.4 %copy-start.2 = (bf16[2,512,512]{1,2,0:T(8,128)(2,1)}, bf16[2,512,512]{1,2,0:T(8,128)(2,1)S(1)}, u32[]{:S(2)}) copy-start(bf16[2,512,512]{1,2,0:T(8,128)(2,1)S(1)} %copy.151) | copy-start | bytes 3145732
  75.8 3.1 copy-start.13
  1293.9 4.6 copy-start
  1307.0 2.0 copy-start.3
  1311.9 2.4 copy-start.11
  1318.9 5.6 copy-start.9
  1318.9 5.6 copy-start.14
  1321.0 12.1 all-to-all-start
Sparse Core Ops, SparseCore 0:
  16.4 1277.4 all-reduce.1
where the time goes:
time: 1360 us; the launch traced here: 1340 us
  waiting for transfers between devices  1250 us (92%)
  matrix products  28 us (2%)
  starting transfers between devices  16.3 us (1%)
  local copies, waits for them, and re-layouts  15.6 us (1%)
  between operations  13.8 us (1%)
    psum x1, waiting for transfers between devices, shards(): summed = lax.psum(gradients, 'ctx')  1210 us
  transfers between devices with their start and end apart: 6, of which 5 were waited for; matrix products, arithmetic and copies ran while one was open for 1% of the time, Pallas kernels for 0%

commit v1 on v0

v1 whole, which is shorter than its diff:
```python
import math

import jax
import jax.numpy as jnp
from jax import lax
from jax.sharding import Mesh, PartitionSpec as P

SWA_DH = 128
WINDOW = 128
NS_ITERS = 2
DH = 512

linear_coef = 3.4445
square_coef = -4.775
quartic_coef = 2.0315
epsilon = 1e-06

CHIPS = ("z", "x", "yh")
PLANE = ("x", "yh")
QUAD = ("core", "yl")


def mat(left, right, dims):
    return lax.dot_general(left, right, (dims, ((), ())), preferred_element_type=jnp.float32)


def refresh(weight, update):
    initial = weight.astype(jnp.float32)
    stepped = initial - update.astype(jnp.float32)
    old_norm = jnp.sqrt(jnp.sum(initial * initial, axis=-2, keepdims=True) + epsilon)
    new_norm = jnp.sqrt(jnp.sum(stepped * stepped, axis=-2, keepdims=True) + epsilon)
    return (stepped * (old_norm / new_norm)).astype(jnp.bfloat16)


def core_exchange(arrays):
    rows = arrays[0].shape[0]
    packed = jnp.stack([a.reshape(rows, 2, DH).transpose(1, 0, 2) for a in arrays], axis=1)
    moved = lax.all_to_all(packed, "core", split_axis=0, concat_axis=0, tiled=True)
    return [moved[:, i].reshape(2 * rows, DH) for i in range(len(arrays))]


def attend(q, k, v, halo, first):
    blocks = q.shape[0] // WINDOW
    heads = q.shape[1] // SWA_DH

    def split(a):
        return a.reshape(-1, WINDOW, heads, SWA_DH)

    keys = split(jnp.concatenate([halo[0], k], axis=0))
    values = split(jnp.concatenate([halo[1], v], axis=0))
    q = split(q)
    scale = 1.0 / math.sqrt(SWA_DH)

    def scores(keys):
        return jnp.einsum("bqhd,bkhd->bhqk", q, keys, preferred_element_type=jnp.float32) * scale

    i = jnp.arange(WINDOW, dtype=jnp.int32)
    older = i[None, :] > i[:, None]
    block = jnp.arange(blocks, dtype=jnp.int32)[:, None, None, None]
    old_scores = jnp.where(older & ((block > 0) | jnp.logical_not(first)), scores(keys[:-1]), -jnp.inf)
    new_scores = jnp.where(jnp.logical_not(older), scores(keys[1:]), -jnp.inf)
    both = jnp.concatenate([old_scores, new_scores], axis=-1)
    peak = jnp.max(both, axis=-1, keepdims=True)
    exponent = jnp.exp(both - peak)
    total = jnp.sum(exponent, axis=-1, keepdims=True)
    probs = (exponent / total).astype(jnp.bfloat16)
    window_values = jnp.concatenate([values[:-1], values[1:]], axis=1)
    result = jnp.einsum("bhqk,bkhd->bqhd", probs, window_values, preferred_element_type=jnp.float32)
    return result.reshape(blocks * WINDOW, heads * SWA_DH)


def shards(fw_q, fw_k, fw_v, fw_lr, fast_gate, fast_up, fast_down, attn_q, attn_k, attn_v):
    rows = fw_k.shape[0]
    core = lax.axis_index("core")
    chip = lax.axis_index(CHIPS)
    gate, up, down = (
        lax.dynamic_index_in_dim(w, core, 0, keepdims=False) for w in (fast_gate, fast_up, fast_down)
    )
    rates = jnp.repeat(fw_lr, DH, axis=1)
    out_grad = (-(rates * fw_v.astype(jnp.float32))).astype(jnp.bfloat16)
    keys, out_grad = core_exchange([fw_k, out_grad])
    nn, nt, tn = ((1,), (0,)), ((1,), (1,)), ((0,), (0,))
    pre_gate = mat(keys, gate, nn)
    pre_up = mat(keys, up, nn)
    sigmoid_gate = jax.nn.sigmoid(pre_gate)
    activated = pre_gate * sigmoid_gate
    hidden = (activated * pre_up).astype(jnp.bfloat16)
    grad_down = mat(hidden, out_grad, tn)
    hidden_grad = mat(out_grad, down, nt)
    slope = sigmoid_gate * (1.0 + pre_gate * (1.0 - sigmoid_gate))
    gate_grad = (hidden_grad * pre_up * slope).astype(jnp.bfloat16)
    up_grad = (hidden_grad * activated).astype(jnp.bfloat16)
    grad_gate = mat(keys, gate_grad, tn)
    grad_up = mat(keys, up_grad, tn)
    partial = jnp.concatenate(
        [g.astype(jnp.bfloat16) for g in (grad_gate, grad_up, grad_down)], axis=0
    )
    plane = lax.axis_size(PLANE)
    depth = lax.axis_size("z")
    part = partial.reshape(plane, -1, DH)
    part = lax.all_to_all(part, PLANE, split_axis=0, concat_axis=0, tiled=True)
    part = jnp.sum(part.astype(jnp.float32), axis=0).astype(jnp.bfloat16).reshape(depth, -1, DH)
    part = lax.all_to_all(part, "z", split_axis=0, concat_axis=0, tiled=True)
    part = jnp.sum(part.astype(jnp.float32), axis=0).astype(jnp.bfloat16)
    part = lax.all_to_all(
        jnp.broadcast_to(part, (depth,) + part.shape), "z", split_axis=0, concat_axis=0, tiled=True
    ).reshape(-1, DH)
    summed = lax.all_to_all(
        jnp.broadcast_to(part, (plane,) + part.shape), PLANE, split_axis=0, concat_axis=0, tiled=True
    ).reshape(3, DH, DH)

    queries, q, k, v = core_exchange([fw_q, attn_q, attn_k, attn_v])
    chips = lax.axis_size(CHIPS)
    halo = lax.ppermute(
        jnp.stack([k[-WINDOW:], v[-WINDOW:]]), CHIPS, [(s, s + 1) for s in range(chips - 1)]
    )
    attended = attend(q, k, v, halo, chip == 0)

    summed = summed.astype(jnp.float32)
    norm_total = jnp.sum(summed * summed, axis=(1, 2), keepdims=True)
    iterate = (summed / jnp.sqrt(norm_total + epsilon)).astype(jnp.bfloat16)
    for _ in range(NS_ITERS):
        gram = jnp.einsum(
            "bij,bkj->bik", iterate, iterate, preferred_element_type=jnp.float32
        ).astype(jnp.bfloat16)
        square = jnp.einsum("bij,bjk->bik", gram, gram, preferred_element_type=jnp.float32)
        polynomial = (square_coef * gram.astype(jnp.float32) + quartic_coef * square).astype(
            jnp.bfloat16
        )
        iterate = (
            linear_coef * iterate.astype(jnp.float32)
            + jnp.einsum("bij,bjk->bik", polynomial, iterate, preferred_element_type=jnp.float32)
        ).astype(jnp.bfloat16)
    renewed = refresh(jnp.stack([gate, up, down]), iterate)
    query_gate = mat(queries, renewed[0], nn)
    query_up = mat(queries, renewed[1], nn)
    query_hidden = (jax.nn.silu(query_gate) * query_up).astype(jnp.bfloat16)
    memory = mat(query_hidden, renewed[2], nn).astype(jnp.bfloat16)
    mixed = (memory.astype(jnp.float32) + attended).astype(jnp.bfloat16)
    moved = lax.all_to_all(
        mixed.reshape(4, -1, DH), QUAD, split_axis=0, concat_axis=0, tiled=True
    )
    moved = moved.reshape(2, 2, -1, DH).transpose(2, 1, 0, 3)
    return moved.reshape(2 * rows // 4, 4 * DH)


def solution(mesh):
    fine = Mesh(mesh.devices.reshape(8, 4, 2, 2, 2), ("z", "x", "yh", "core", "yl"))
    ctx = ("z", "x", "yh", "core")
    wide = P(ctx, "yl")
    weight = P("yl", None, None)
    in_specs = (wide, wide, wide, wide, weight, weight, weight, wide, wide, wide)
    out_specs = P(ctx + ("yl",), None)
    return jax.shard_map(shards, mesh=fine, in_specs=in_specs, out_specs=out_specs, check_vma=False)
```

time: 1360 us -> 171 us (0.13); the launches traced: 1340 us -> 169 us
  waiting for transfers between devices: 1250 us -> 33.8 us
  local copies, waits for them, and re-layouts: 15.6 us -> 43.8 us
  starting transfers between devices: 16.3 us -> 34.7 us
    psum x1 -> x0, waiting for transfers between devices: 1210 us -> none  [shards(): summed = lax.psum(gradients, 'ctx')]
    all_to_all x4 -> x6, starting transfers between devices: 14.1 us -> 32.2 us  [the longest x1 8.48 us: shards(): part = lax.all_to_all(part, 'z', split_axis=0, concat_axis=0, tiled=True)]
    unnamed x35 -> x59, local copies, waits for them, and re-layouts: 6.38 us -> 20.4 us
    all_to_all x4 -> x6, waiting for transfers between devices: 42.9 us -> 33.8 us  [the longest x1 18.7 us: shards(): part = lax.all_to_all(part, PLANE, split_axis=0, concat_axis=0, tiled=True)]
  transfers between devices with their start and end apart: 6 -> 7, of which waited for: 5 -> 3; matrix products, arithmetic and copies ran while one was open for 1% -> 32% of each run, Pallas kernels for 0% -> 0%
where the time goes in v1:
time: 171 us; the launch traced here: 169 us
  local copies, waits for them, and re-layouts  43.8 us (26%)
  starting transfers between devices  34.7 us (20%)
  waiting for transfers between devices  33.8 us (20%)
  matrix products  33.3 us (19%)
  other arithmetic  12.2 us (7%)
  blocking collectives  11.2 us (7%)
    unnamed x59, local copies, waits for them, and re-layouts  20.4 us
    all_to_all x1, waiting for transfers between devices, shards(): part = lax.all_to_all(part, PLANE, split_axis=0, concat_axis=0, tiled=True)  18.7 us
    dot_general x2, matrix products, shards(): jnp.einsum('bij,bjk->bik', polynomial, iterate, preferred_element_type=jn...  11.8 us
    dot_general x8, matrix products, mat(): lax.dot_general(left, right, (dims, ((), ())), preferred_element_type=jnp...  11.4 us
    all_to_all x1, blocking collectives, shards(): lax.all_to_all(mixed.reshape(4, -1, DH), QUAD, split_axis=0, concat_axis=...  11.2 us
    all_to_all x1, starting transfers between devices, shards(): part = lax.all_to_all(part, 'z', split_axis=0, concat_axis=0, tiled=True)  8.48 us
    all_to_all x1, waiting for transfers between devices, shards(): lax.all_to_all(jnp.broadcast_to(part, (depth,) + part.shape), 'z', split_...  8.22 us
    all_to_all x1, starting transfers between devices, shards(): part = lax.all_to_all(part, PLANE, split_axis=0, concat_axis=0, tiled=True)  7.43 us
  transfers between devices with their start and end apart: 7, of which 3 were waited for; matrix products, arithmetic and copies ran while one was open for 32% of the time, Pallas kernels for 0%

profile of v1, /device:TPU:4, one launch (start us, length us, event | category | flops | bytes accessed | tf_op | source)
XLA Modules:
  0.0 169.4 jit_solution(9151911201014402773)
XLA Ops:
  0.0 1.3 copy.78
  1.4 1.2 copy.77
  3.9 3.6 %all-to-all-start.1 = ((bf16[2,2,256,512]{2,3,1,0:T(8,128)(2,1)}), bf16[2,2,256,512]{2,3,1,0:T(8,128)(2,1)S(1)}, u32[]{:S(2)}, u32[]{:S(2)}) async-start(bf16[2,2,256,512]{2,3,1,0:T(8,128)(2,1)} %copy.79), calls=%async_computation.1 | async-start | bytes 2097152 | tf_op jit(solution)/shard_map/all_to_all | solution.py:38
  7.7 1.2 copy.71
  9.0 2.1 %copy.72 = bf16[256,1024]{0,1:T(8,128)(2,1)} copy(bf16[256,1024]{1,0:T(8,128)(2,1)} %param.17) | data formatting | bytes 1048576 | tf_op args[7]
  11.1 2.0 %copy.73 = bf16[256,1024]{0,1:T(8,128)(2,1)} copy(bf16[256,1024]{1,0:T(8,128)(2,1)} %param.18) | data formatting | bytes 1048576 | tf_op args[8]
  13.1 1.5 pad_maximum_fusion
  14.6 1.4 copy.75
  17.0 3.8 %all-to-all-start = ((bf16[2,4,256,512]{2,3,1,0:T(8,128)(2,1)}), bf16[2,4,256,512]{2,3,1,0:T(8,128)(2,1)S(1)}, u32[]{:S(2)}, u32[]{:S(2)}) async-start(bf16[2,4,256,512]{2,3,1,0:T(8,128)(2,1)} %copy.75), calls=%async_computation | async-start | bytes 4194304 | tf_op jit(solution)/shard_map/all_to_all | solution.py:38
  20.8 2.2 %fusion.46 = (bf16[2,1,256,512]{2,3,1,0:T(8,128)(2,1)}, bf16[2,1,256,512]{2,3,1,0:T(8,128)(2,1)}) fusion(bf16[2,2,256,512]{2,3,1,0:T(8,128)(2,1)} %copy-done.9), kind=kLoop, calls=%fused_computation.94 | loop fusion | bytes 2097152 | tf_op jit(solution)/shard_map/slice | solution.py:39
  23.0 2.1 %copy.96 = bf16[2,1,256,512]{3,2,0,1:T(8,128)(2,1)} copy(bf16[2,1,256,512]{2,3,1,0:T(8,128)(2,1)} %get-tuple-element.11) | data formatting | bytes 1048576
  25.1 2.3 %constant_dynamic-slice_fusion = (bf16[1,512,512]{2,1,0:T(8,128)(2,1)}, bf16[1,512,512]{2,1,0:T(8,128)(2,1)S(1)}) fusion(bf16[2,512,512]{2,1,0:T(8,128)(2,1)} %param.16, s32[]{:T(128)S(6)} %select_n.14, bf16[2,512,512]{2,1,0:T(8,128)(2,1)} %param.15), kind=kLoop, calls=%fused_computation.79 | loop fusion | bytes 2097156 | tf_op jit(solution)/shard_map/jit(dynamic_index_in_dim)/dynamic_slice | solution.py:77
  27.4 1.4 fusion.23
  28.8 1.4 fusion.21
  30.3 2.0 %copy.97 = bf16[2,1,256,512]{3,2,0,1:T(8,128)(2,1)} copy(bf16[2,1,256,512]{2,3,1,0:T(8,128)(2,1)} %get-tuple-element.12) | data formatting | bytes 1048576
  32.3 1.8 %fusion.25 = f32[512,512]{1,0:T(8,128)S(1)} fusion(bf16[512,512]{1,0:T(8,128)(2,1)} %bitcast.128, bf16[1,512,512]{2,1,0:T(8,128)(2,1)} %get-tuple-element.22), kind=kOutput, calls=%fused_computation.61 | convolution fusion | flops 268435456 | bytes 2097152 | tf_op jit(solution)/shard_map/dot_general | solution.py:24
  34.2 1.8 %convolution_convert_fusion.3 = bf16[512,512]{1,0:T(8,128)(2,1)S(1)} fusion(bf16[512,512]{1,0:T(8,128)(2,1)S(1)} %bitcast.129, f32[512,512]{1,0:T(8,128)} %fusion.23, f32[512,512]{1,0:T(8,128)S(1)} %copy-done.17), kind=kOutput, calls=%fused_computation.27 | convolution fusion | flops 270270464 | bytes 3145728 | tf_op jit(solution)/shard_map/dot_general | solution.py:24
  37.3 1.3 pad_maximum_fusion.2
  38.5 7.4 %all-to-all-start.2 = ((bf16[8,192,512]{2,1,0:T(8,128)(2,1)}), bf16[8,192,512]{2,1,0:T(8,128)(2,1)}, u32[]{:S(2)}, u32[]{:S(2)}) async-start(bf16[8,192,512]{2,1,0:T(8,128)(2,1)} %bitcast.115), calls=%async_computation.2 | async-start | bytes 3145728 | tf_op jit(solution)/shard_map/all_to_all | solution.py:101
  46.0 1.4 fusion.45
  47.3 1.3 copy.98
  48.6 1.4 copy.99
  50.1 18.7 %all-to-all-done.2 = bf16[8,192,512]{2,1,0:T(8,128)(2,1)} async-done(((bf16[8,192,512]{2,1,0:T(8,128)(2,1)}), bf16[8,192,512]{2,1,0:T(8,128)(2,1)}, u32[]{:S(2)}, u32[]{:S(2)}) %all-to-all-start.2) | async-done | bytes 1572896 | tf_op jit(solution)/shard_map/all_to_all | solution.py:101
  68.7 2.4 %reduce_sum.67 = bf16[192,512]{1,0:T(8,128)(2,1)} reduce(bf16[8,192,512]{2,1,0:T(8,128)(2,1)} %all-to-all-done.2, bf16[]{:T(256)} %constant.41.clone.1), dimensions={0}, to_apply=%region_0.1 | reduce | flops 688128 | bytes 1769474 | tf_op jit(solution)/shard_map/reduce_sum | solution.py:102
  71.1 8.5 %all-to-all-start.3 = ((bf16[8,24,512]{2,1,0:T(8,128)(2,1)}), bf16[8,24,512]{2,1,0:T(8,128)(2,1)S(1)}, u32[]{:S(2)}, u32[]{:S(2)}) async-start(bf16[8,24,512]{2,1,0:T(8,128)(2,1)} %bitcast.26), calls=%async_computation.3 | async-start | bytes 393216 | tf_op jit(solution)/shard_map/all_to_all | solution.py:103
  80.3 2.5 %collective-permute-start = (bf16[2,128,512]{2,1,0:T(8,128)(2,1)}, bf16[2,128,512]{2,1,0:T(8,128)(2,1)}, u32[]{:S(2)}, u32[]{:S(2)}) collective-permute-start(bf16[2,128,512]{2,1,0:T(8,128)(2,1)} %pad_maximum_fusion.6), channel_id=1, source_target_pairs={{0,4},{4,8},{8,12},{12,16},{16,20},{20,24},{24,28},{28,32},{32,36}... | collective-permute-start | bytes 786440 | tf_op jit(solution)/shard_map/ppermute | solution.py:114
  83.4 6.9 %all-to-all-done.3 = bf16[8,24,512]{2,1,0:T(8,128)(2,1)S(1)} async-done(((bf16[8,24,512]{2,1,0:T(8,128)(2,1)}), bf16[8,24,512]{2,1,0:T(8,128)(2,1)S(1)}, u32[]{:S(2)}, u32[]{:S(2)}) %all-to-all-start.3) | async-done | bytes 196640 | tf_op jit(solution)/shard_map/all_to_all | solution.py:103
  91.0 3.4 %all-to-all-start.4 = ((bf16[8,24,512]{2,1,0:T(8,128)(2,1)}), bf16[8,24,512]{2,1,0:T(8,128)(2,1)S(1)}, u32[]{:S(2)}, u32[]{:S(2)}) async-start(bf16[8,24,512]{2,1,0:T(8,128)(2,1)} %broadcast_in_dim.37), calls=%async_computation.4 | async-start | bytes 393216 | tf_op jit(solution)/shard_map/all_to_all | solution.py:105
  94.4 1.5 fusion.48
  95.9 8.2 %all-to-all-done.4 = bf16[8,24,512]{2,1,0:T(8,128)(2,1)S(1)} async-done(((bf16[8,24,512]{2,1,0:T(8,128)(2,1)}), bf16[8,24,512]{2,1,0:T(8,128)(2,1)S(1)}, u32[]{:S(2)}, u32[]{:S(2)}) %all-to-all-start.4) | async-done | bytes 196640 | tf_op jit(solution)/shard_map/all_to_all | solution.py:105
  104.1 1.3 broadcast_in_dim.38
  105.4 5.6 %all-to-all-start.5 = ((bf16[8,192,512]{2,1,0:T(8,128)(2,1)}), bf16[8,192,512]{2,1,0:T(8,128)(2,1)S(1)}, u32[]{:S(2)}, u32[]{:S(2)}) async-start(bf16[8,192,512]{2,1,0:T(8,128)(2,1)} %broadcast_in_dim.38), calls=%async_computation.5 | async-start | bytes 3145728 | tf_op jit(solution)/shard_map/all_to_all | solution.py:108
  112.0 2.0 %copy.95 = bf16[2,1,256,512]{3,2,0,1:T(8,128)(2,1)} copy(bf16[2,1,256,512]{2,3,1,0:T(8,128)(2,1)} %get-tuple-element.9) | data formatting | bytes 1048576
  114.0 2.1 %copy.85 = bf16[4,128,4,128]{1,3,2,0:T(8,128)(2,1)} copy(bf16[4,128,4,128]{3,2,1,0:T(4,128)(2,1)} %slice.72) | data formatting | bytes 1048576 | tf_op jit(solution)/shard_map/slice | solution.py:67
  117.1 1.8 %pad_maximum_fusion.4 = bf16[512,512]{1,0:T(8,128)(2,1)} fusion(bf16[512,512]{1,0:T(8,128)(2,1)} %bitcast.119, bf16[128,512]{1,0:T(8,128)(2,1)S(1)} %get-tuple-element.13), kind=kLoop, calls=%fused_computation.51 | loop fusion | flops 1048576 | bytes 1179648 | tf_op jit(solution)/shard_map/concatenate | solution.py:49
  118.9 2.0 %slice.76 = bf16[4,128,4,128]{3,2,1,0:T(4,128)(2,1)} reshape(bf16[512,512]{1,0:T(8,128)(2,1)} %pad_maximum_fusion.4) | data formatting | bytes 1048576 | tf_op jit(solution)/shard_map/slice | solution.py:60
  124.0 1.8 %fusion.47 = (f32[4,4,128]{2,1,0:T(4,128)S(1)}, f32[4,4,128,128]{2,3,1,0:T(8,128)S(1)}) fusion(bf16[4,128,4,128]{3,2,1,0:T(4,128)(2,1)} %slice.76, bf16[4,128,4,128]{3,2,1,0:T(4,128)(2,1)} %copy-done.20, pred[4,128,128]{1,2,0:T(8,128)(4,1)S(1)} %broadcast_and_fusion), kind=kOutput, calls=%fused_computation.95 | convolution fusion | flops 67893248 | bytes 2170880 | tf_op jit(solution)/shard_map/bqhd,bkhd->bhqk/dot_general | solution.py:55
  126.2 1.5 convolution_bitcast_fusion
  127.7 2.6 %copy.92 = f32[4,128,4,128]{3,2,1,0:T(4,128)} copy(f32[4,128,4,128]{1,3,2,0:T(8,128)} %convolution_bitcast_fusion) | data formatting | bytes 2097152 | tf_op jit(solution)/shard_map/bhqk,bkhd->bqhd/transpose | solution.py:68
  131.4 1.2 copy-done.14
  133.6 4.8 %add_convert_fusion.2 = bf16[3,512,512]{2,1,0:T(8,128)(2,1)} fusion(bf16[3,512,512]{2,1,0:T(8,128)(2,1)} %copy-done.14, bf16[3,512,512]{2,1,0:T(8,128)(2,1)S(1)} %convolution_convert_fusion.1), kind=kOutput, calls=%fused_computation.7 | convolution fusion | flops 1617690624 | bytes 4718592 | tf_op jit(solution)/shard_map/bij,bjk->bik/dot_general | solution.py:132
  138.5 4.2 %convolution_convert_fusion = bf16[3,512,512]{2,1,0:T(8,128)(2,1)} fusion(bf16[3,512,512]{2,1,0:T(8,128)(2,1)} %add_convert_fusion.2), kind=kOutput, calls=%fused_computation.15 | convolution fusion | flops 806092800 | bytes 3145728 | tf_op jit(solution)/shard_map/bij,bkj->bik/dot_general | solution.py:123
  142.7 7.0 %fusion = (f32[3,512]{1,0:T(4,128)S(1)}, f32[3,512]{1,0:T(4,128)S(1)}, bf16[3,512,512]{2,1,0:T(8,128)(2,1)}) fusion(bf16[1,512,512]{2,1,0:T(8,128)(2,1)S(1)} %copy-done.2, bf16[1,512,512]{2,1,0:T(8,128)(2,1)S(1)} %copy-done.4, bf16[1,512,512]{2,1,0:T(8,128)(2,1)S(1)} %copy-done.6, bf16[3,512,512]{2,1,0:T(8,128)(2,1)} %add_convert_fusion.2, ...), kind=kOutput, calls=%fused_computation.2 | convolution fusion | flops 1627124736 | bytes 6303744 | tf_op jit(solution)/shard_map/bij,bjk->bik/dot_general | solution.py:132
  149.7 1.9 %multiply_convert_fusion = bf16[3,512,512]{2,1,0:T(8,128)(2,1)S(1)} fusion(bf16[3,512,512]{2,1,0:T(8,128)(2,1)} %get-tuple-element.19, f32[3,512]{1,0:T(4,128)S(1)} %rsqrt_multiply_fusion, bf16[1,512,512]{2,1,0:T(8,128)(2,1)S(1)} %copy-done.2, bf16[1,512,512]{2,1,0:T(8,128)(2,1)S(1)} %copy-done.4, bf16[1,512,512]{2,1,0:T(8,128)(2,1)S(1)} %copy-done.6), kind=kLoop, calls=%fused_computation.3 | loop fusion | flops 5505024 | bytes 4724736 | tf_op jit(solution)/shard_map/convert_element_type | solution.py:32
  152.8 1.4 fusion.20
  154.2 2.3 %fusion.7 = bf16[512,512]{1,0:T(8,128)(2,1)S(1)} fusion(bf16[512,512]{1,0:T(8,128)(2,1)S(1)} %bitcast.127, f32[64,8,4,128]{3,2,1,0:T(4,128)S(1)} %bitcast.136, f32[512,512]{1,0:T(8,128)} %fusion.20, bf16[3,512,512]{2,1,0:T(8,128)(2,1)} %copy-done.10), kind=kOutput, calls=%fused_computation.32 | convolution fusion | flops 539492352 | bytes 4194304 | tf_op jit(solution)/shard_map/dot_general | solution.py:24
  156.5 11.2 %all_to_all.35 = bf16[4,128,512]{2,1,0:T(8,128)(2,1)S(1)} all-to-all(bf16[4,128,512]{2,1,0:T(8,128)(2,1)S(1)} %bitcast.138), channel_id=1, replica_groups=mesh['z'=8,'x'=4,'yh'=2,'core'=2,'yl'=2] {'core','yl'}, dimensions={0} | all-to-all | bytes 1048576 | tf_op jit(solution)/shard_map/all_to_all | solution.py:140
  168.3 1.2 reshape.118
  (84 shorter events, 15.1 us)
Async XLA Ops:
  0.0 25.1 %copy-start = (bf16[2,512,512]{2,1,0:T(8,128)(2,1)S(1)}, bf16[2,512,512]{2,1,0:T(8,128)(2,1)}, u32[]{:S(2)}) copy-start(bf16[2,512,512]{2,1,0:T(8,128)(2,1)} %param.14) | copy-start | bytes 3145732
  0.0 2.6 %copy-start.23 = (f32[256,2]{0,1:T(2,128)S(1)}, f32[256,2]{0,1:T(2,128)}, u32[]{:S(2)}) copy-start(f32[256,2]{0,1:T(2,128)} %param.13) | copy-start | bytes 6148
  2.9 4.7 %copy-start.19 = (bf16[256,1024]{1,0:T(8,128)(2,1)S(1)}, bf16[256,1024]{1,0:T(8,128)(2,1)}, u32[]{:S(2)}) copy-start(bf16[256,1024]{1,0:T(8,128)(2,1)} %param.19) | copy-start | bytes 1572868
  3.9 12.1 %all-to-all-start.1 = ((bf16[2,2,256,512]{2,3,1,0:T(8,128)(2,1)}), bf16[2,2,256,512]{2,3,1,0:T(8,128)(2,1)S(1)}, u32[]{:S(2)}, u32[]{:S(2)}) async-start(bf16[2,2,256,512]{2,3,1,0:T(8,128)(2,1)} %copy.79), calls=%async_computation.1 | async-start | bytes 2097152 | tf_op jit(solution)/shard_map/all_to_all | solution.py:38
  16.0 1.0 copy-start.9
  17.0 21.6 %all-to-all-start = ((bf16[2,4,256,512]{2,3,1,0:T(8,128)(2,1)}), bf16[2,4,256,512]{2,3,1,0:T(8,128)(2,1)S(1)}, u32[]{:S(2)}, u32[]{:S(2)}) async-start(bf16[2,4,256,512]{2,3,1,0:T(8,128)(2,1)} %copy.75), calls=%async_computation | async-start | bytes 4194304 | tf_op jit(solution)/shard_map/all_to_all | solution.py:38
  25.1 2.4 %copy-start.7 = (bf16[2,1,256,512]{3,2,0,1:T(8,128)(2,1)S(1)}, bf16[2,1,256,512]{3,2,0,1:T(8,128)(2,1)}, u32[]{:S(2)}) copy-start(bf16[2,1,256,512]{3,2,0,1:T(8,128)(2,1)} %copy.96) | copy-start | bytes 1572868
  25.1 3.7 %copy-start.5 = (bf16[1,512,512]{2,1,0:T(8,128)(2,1)}, bf16[1,512,512]{2,1,0:T(8,128)(2,1)S(1)}, u32[]{:S(2)}) copy-start(bf16[1,512,512]{2,1,0:T(8,128)(2,1)S(1)} %constant_dynamic-slice_fusion.2) | copy-start | bytes 1572868
  27.4 2.9 %copy-start.3 = (bf16[1,512,512]{2,1,0:T(8,128)(2,1)}, bf16[1,512,512]{2,1,0:T(8,128)(2,1)S(1)}, u32[]{:S(2)}) copy-start(bf16[1,512,512]{2,1,0:T(8,128)(2,1)S(1)} %get-tuple-element.23) | copy-start | bytes 1572868
  32.3 1.8 %copy-start.12 = (bf16[2,1,256,512]{3,2,0,1:T(8,128)(2,1)S(1)}, bf16[2,1,256,512]{3,2,0,1:T(8,128)(2,1)}, u32[]{:S(2)}) copy-start(bf16[2,1,256,512]{3,2,0,1:T(8,128)(2,1)} %copy.97) | copy-start | bytes 1572868
  32.3 1.8 %copy-start.17 = (f32[512,512]{1,0:T(8,128)S(1)}, f32[512,512]{1,0:T(8,128)}, u32[]{:S(2)}) copy-start(f32[512,512]{1,0:T(8,128)} %fusion.21) | copy-start | bytes 3145732
  34.1 1.9 %copy-start.8 = (bf16[2,1,256,512]{3,2,0,1:T(8,128)(2,1)S(1)}, bf16[2,1,256,512]{3,2,0,1:T(8,128)(2,1)}, u32[]{:S(2)}) copy-start(bf16[2,1,256,512]{3,2,0,1:T(8,128)(2,1)} %copy.96) | copy-start | bytes 1572868
  34.1 1.9 %copy-start.18 = (f32[512,512]{1,0:T(8,128)S(1)}, f32[512,512]{1,0:T(8,128)}, u32[]{:S(2)}) copy-start(f32[512,512]{1,0:T(8,128)} %fusion.23) | copy-start | bytes 3145732
  38.5 30.2 %all-to-all-start.2 = ((bf16[8,192,512]{2,1,0:T(8,128)(2,1)}), bf16[8,192,512]{2,1,0:T(8,128)(2,1)}, u32[]{:S(2)}, u32[]{:S(2)}) async-start(bf16[8,192,512]{2,1,0:T(8,128)(2,1)} %bitcast.115), calls=%async_computation.2 | async-start | bytes 3145728 | tf_op jit(solution)/shard_map/all_to_all | solution.py:101
  48.6 34.2 %copy-start.1 = (bf16[2,1,256,512]{3,2,0,1:T(8,128)(2,1)}, bf16[2,1,256,512]{3,2,0,1:T(8,128)(2,1)S(1)}, u32[]{:S(2)}) copy-start(bf16[2,1,256,512]{3,2,0,1:T(8,128)(2,1)S(1)} %copy.98) | copy-start | bytes 1572868
  50.0 32.9 %copy-start.13 = (bf16[2,1,256,512]{2,3,1,0:T(8,128)(2,1)S(1)}, bf16[2,1,256,512]{2,3,1,0:T(8,128)(2,1)}, u32[]{:S(2)}) copy-start(bf16[2,1,256,512]{2,3,1,0:T(8,128)(2,1)} %get-tuple-element.7) | copy-start | bytes 1572868
  71.1 19.2 %all-to-all-start.3 = ((bf16[8,24,512]{2,1,0:T(8,128)(2,1)}), bf16[8,24,512]{2,1,0:T(8,128)(2,1)S(1)}, u32[]{:S(2)}, u32[]{:S(2)}) async-start(bf16[8,24,512]{2,1,0:T(8,128)(2,1)} %bitcast.26), calls=%async_computation.3 | async-start | bytes 393216 | tf_op jit(solution)/shard_map/all_to_all | solution.py:103
  80.3 35.8 %collective-permute-start = (bf16[2,128,512]{2,1,0:T(8,128)(2,1)}, bf16[2,128,512]{2,1,0:T(8,128)(2,1)}, u32[]{:S(2)}, u32[]{:S(2)}) collective-permute-start(bf16[2,128,512]{2,1,0:T(8,128)(2,1)} %pad_maximum_fusion.6), channel_id=1, source_target_pairs={{0,4},{4,8},{8,12},{12,16},{16,20},{20,24},{24,28},{28,32},{32,36}... | collective-permute-start | bytes 786440 | tf_op jit(solution)/shard_map/ppermute | solution.py:114
  83.3 22.1 %copy-start.20 = (bf16[4,128,4,128]{3,2,1,0:T(4,128)(2,1)}, bf16[4,128,4,128]{3,2,1,0:T(4,128)(2,1)S(1)}, u32[]{:S(2)}) copy-start(bf16[4,128,4,128]{3,2,1,0:T(4,128)(2,1)S(1)} %reshape_reshape_squeeze.3) | copy-start | bytes 1572868
  91.0 13.1 %all-to-all-start.4 = ((bf16[8,24,512]{2,1,0:T(8,128)(2,1)}), bf16[8,24,512]{2,1,0:T(8,128)(2,1)S(1)}, u32[]{:S(2)}, u32[]{:S(2)}) async-start(bf16[8,24,512]{2,1,0:T(8,128)(2,1)} %broadcast_in_dim.37), calls=%async_computation.4 | async-start | bytes 393216 | tf_op jit(solution)/shard_map/all_to_all | solution.py:105
  105.4 24.9 %all-to-all-start.5 = ((bf16[8,192,512]{2,1,0:T(8,128)(2,1)}), bf16[8,192,512]{2,1,0:T(8,128)(2,1)S(1)}, u32[]{:S(2)}, u32[]{:S(2)}) async-start(bf16[8,192,512]{2,1,0:T(8,128)(2,1)} %broadcast_in_dim.38), calls=%async_computation.5 | async-start | bytes 3145728 | tf_op jit(solution)/shard_map/all_to_all | solution.py:108
  124.0 1.9 %copy-start.15 = (f32[4,4,128,128]{2,3,1,0:T(8,128)S(1)}, f32[4,4,128,128]{2,3,1,0:T(8,128)}, u32[]{:S(2)}) copy-start(f32[4,4,128,128]{2,3,1,0:T(8,128)} %get-tuple-element.18) | copy-start | bytes 3145732
  124.0 2.2 %copy-start.21 = (bf16[4,128,4,128]{1,3,2,0:T(8,128)(2,1)S(1)}, bf16[4,128,4,128]{1,3,2,0:T(8,128)(2,1)}, u32[]{:S(2)}) copy-start(bf16[4,128,4,128]{1,3,2,0:T(8,128)(2,1)} %copy.85) | copy-start | bytes 1572868
  124.0 2.2 %copy-start.22 = (bf16[4,128,4,128]{1,3,2,0:T(8,128)(2,1)S(1)}, bf16[4,128,4,128]{1,3,2,0:T(8,128)(2,1)}, u32[]{:S(2)}) copy-start(bf16[4,128,4,128]{1,3,2,0:T(8,128)(2,1)} %copy.84) | copy-start | bytes 1572868
  131.4 1.2 copy-start.14
  138.5 4.2 %copy-start.2 = (bf16[1,512,512]{2,1,0:T(8,128)(2,1)S(1)}, bf16[1,512,512]{2,1,0:T(8,128)(2,1)}, u32[]{:S(2)}) copy-start(bf16[1,512,512]{2,1,0:T(8,128)(2,1)} %get-tuple-element.22) | copy-start | bytes 1572868
  138.5 4.2 %copy-start.4 = (bf16[1,512,512]{2,1,0:T(8,128)(2,1)S(1)}, bf16[1,512,512]{2,1,0:T(8,128)(2,1)}, u32[]{:S(2)}) copy-start(bf16[1,512,512]{2,1,0:T(8,128)(2,1)} %copy-done.3) | copy-start | bytes 1572868
  138.5 4.2 %copy-start.6 = (bf16[1,512,512]{2,1,0:T(8,128)(2,1)S(1)}, bf16[1,512,512]{2,1,0:T(8,128)(2,1)}, u32[]{:S(2)}) copy-start(bf16[1,512,512]{2,1,0:T(8,128)(2,1)} %copy-done.5) | copy-start | bytes 1572868
  149.7 3.1 %copy-start.11 = (bf16[2,1,256,512]{3,2,0,1:T(8,128)(2,1)S(1)}, bf16[2,1,256,512]{3,2,0,1:T(8,128)(2,1)}, u32[]{:S(2)}) copy-start(bf16[2,1,256,512]{3,2,0,1:T(8,128)(2,1)} %copy.95) | copy-start | bytes 1572868
  151.6 1.2 copy-start.10
  151.6 2.6 %copy-start.16 = (f32[4,128,4,128]{3,2,1,0:T(4,128)S(1)}, f32[4,128,4,128]{3,2,1,0:T(4,128)}, u32[]{:S(2)}) copy-start(f32[4,128,4,128]{3,2,1,0:T(4,128)} %copy.92) | copy-start | bytes 3145732

commit v2 on v1

v2 whole, which is shorter than its diff:
```python
import math

import jax
import jax.numpy as jnp
from jax import lax
from jax.experimental import pallas as pl
from jax.experimental.pallas import tpu as pltpu
from jax.sharding import Mesh, PartitionSpec as P

SWA_DH = 128
WINDOW = 128
NS_ITERS = 2
DH = 512
HALF = 256

linear_coef = 3.4445
square_coef = -4.775
quartic_coef = 2.0315
epsilon = 1e-06

CHIPS = ("z", "x", "yh")
PLANE = ("x", "yh")
QUAD = ("core", "yl")

BF = jnp.bfloat16
F32 = jnp.float32
NN, NT, TN = ((1,), (0,)), ((1,), (1,)), ((0,), (0,))


def mat(left, right, dims):
    return lax.dot_general(left, right, (dims, ((), ())), preferred_element_type=F32)


def shape(dims, dtype=BF):
    return jax.ShapeDtypeStruct(dims, dtype)


def cost(flops, nbytes, trans=0):
    return pl.CostEstimate(flops=flops, bytes_accessed=nbytes, transcendentals=trans)


def pack_grad_body(k_ref, v_ref, lr_ref, out_ref):
    head = pl.program_id(0)
    rows = k_ref.shape[0]
    rates = jnp.where(head == 0, lr_ref[0:1, :], lr_ref[1:2, :])
    rates = jnp.broadcast_to(rates, (SWA_DH, rows)).T
    out_ref[0, 0] = k_ref[...]
    for j in range(0, DH, SWA_DH):
        cols = slice(j, j + SWA_DH)
        out_ref[0, 1, :, cols] = (-(rates * v_ref[:, cols].astype(F32))).astype(BF)


def pack_grad(fw_k, fw_v, fw_lr):
    rows = fw_k.shape[0]
    wide = pl.BlockSpec((rows, DH), lambda h: (0, h))
    return pl.pallas_call(
        pack_grad_body,
        grid=(2,),
        in_specs=[wide, wide, pl.BlockSpec((2, rows), lambda h: (0, 0))],
        out_specs=pl.BlockSpec((1, 2, rows, DH), lambda h: (h, 0, 0, 0)),
        out_shape=shape((2, 2, rows, DH)),
        cost_estimate=cost(rows * 1024, 8 * rows * 1024),
        name="pack_grad",
    )(fw_k, fw_v, fw_lr.T)


def pack_rest_body(a_ref, b_ref, c_ref, d_ref, out_ref):
    for i, ref in enumerate((a_ref, b_ref, c_ref, d_ref)):
        out_ref[0, i] = ref[...]


def pack_rest(arrays):
    rows = arrays[0].shape[0]
    wide = pl.BlockSpec((rows, DH), lambda h: (0, h))
    return pl.pallas_call(
        pack_rest_body,
        grid=(2,),
        in_specs=[wide] * 4,
        out_specs=pl.BlockSpec((1, 4, rows, DH), lambda h: (h, 0, 0, 0)),
        out_shape=shape((2, 4, rows, DH)),
        cost_estimate=cost(0, 16 * rows * 1024),
        name="pack_rest",
    )(*arrays)


def grads_body(core_ref, moved_ref, gate_ref, up_ref, down_ref, out_ref):
    del core_ref
    half = pl.program_id(0)
    keys = moved_ref[:, 0].reshape(-1, DH)
    out_grad = moved_ref[:, 1].reshape(-1, DH)
    pre_gate = mat(keys, gate_ref[0], NN)
    pre_up = mat(keys, up_ref[0], NN)
    hidden_grad = mat(out_grad, down_ref[0], NT)
    sigmoid_gate = jax.nn.sigmoid(pre_gate)
    activated = pre_gate * sigmoid_gate
    hidden = (activated * pre_up).astype(BF)
    slope = sigmoid_gate * (1.0 + pre_gate * (1.0 - sigmoid_gate))
    gate_grad = (hidden_grad * pre_up * slope).astype(BF)
    up_grad = (hidden_grad * activated).astype(BF)
    grad_gate = mat(keys, gate_grad, TN).astype(BF)
    grad_up = mat(keys, up_grad, TN).astype(BF)
    grad_down = mat(hidden, out_grad, TN).astype(BF)
    for h in range(2):

        @pl.when(half == h)
        def _():
            cols = slice(h * HALF, (h + 1) * HALF)
            out_ref[0, :, cols] = grad_gate
            out_ref[1, :, cols] = grad_up
            out_ref[2, cols, :] = grad_down


def grads(core, moved, gate, up, down):
    tokens = moved.shape[0] * moved.shape[2]
    wide = pl.BlockSpec((1, DH, HALF), lambda h, c: (c[0], 0, h))
    return pl.pallas_call(
        grads_body,
        grid_spec=pltpu.PrefetchScalarGridSpec(
            num_scalar_prefetch=1,
            grid=(2,),
            in_specs=[
                pl.BlockSpec(moved.shape, lambda h, c: (0, 0, 0, 0)),
                wide,
                wide,
                pl.BlockSpec((1, HALF, DH), lambda h, c: (c[0], h, 0)),
            ],
            out_specs=pl.BlockSpec((3, DH, DH), lambda h, c: (0, 0, 0)),
        ),
        out_shape=shape((3, DH, DH)),
        cost_estimate=cost(12 * tokens * DH * DH, 8 * DH * DH * 2, tokens * DH),
        name="grads",
    )(core, moved, gate, up, down)


def sum_body(in_ref, out_ref):
    total = in_ref[0].astype(F32)
    for i in range(1, in_ref.shape[0]):
        total += in_ref[i].astype(F32)
    out_ref[...] = total.astype(BF)


def summed(parts, steps):
    count, rows, cols = parts.shape
    return pl.pallas_call(
        sum_body,
        grid=(steps,),
        in_specs=[pl.BlockSpec((count, rows // steps, cols), lambda i: (0, i, 0))],
        out_specs=pl.BlockSpec((rows // steps, cols), lambda i: (i, 0)),
        out_shape=shape((rows, cols)),
        cost_estimate=cost(count * rows * cols, 2 * count * rows * cols),
        name="plane_sum",
    )(parts)


def sum_spread_body(in_ref, out_ref):
    total = in_ref[0].astype(F32)
    for i in range(1, in_ref.shape[0]):
        total += in_ref[i].astype(F32)
    total = total.astype(BF)
    for i in range(out_ref.shape[0]):
        out_ref[i] = total


def sum_spread(parts):
    return pl.pallas_call(
        sum_spread_body,
        out_shape=shape(parts.shape),
        cost_estimate=cost(parts.size, 4 * parts.size),
        name="depth_sum",
    )(parts)


def spread_body(in_ref, out_ref, sems):
    copies = [
        pltpu.make_async_copy(in_ref, out_ref.at[i], sems.at[i]) for i in range(out_ref.shape[0])
    ]
    for copy in copies:
        copy.start()
    for copy in copies:
        copy.wait()


def spread(part, count):
    return pl.pallas_call(
        spread_body,
        in_specs=[pl.BlockSpec(memory_space=pltpu.VMEM)],
        out_specs=pl.BlockSpec(memory_space=pl.ANY),
        out_shape=shape((count,) + part.shape),
        scratch_shapes=[pltpu.SemaphoreType.DMA((count,))],
        cost_estimate=cost(0, 2 * (count + 1) * part.size),
        name="spread",
    )(part)


def attend_body(chip_ref, q_ref, k_ref, v_ref, halo_ref, out_ref):
    scale = 1.0 / math.sqrt(SWA_DH)
    row = lax.broadcasted_iota(jnp.int32, (WINDOW, WINDOW), 0)
    col = lax.broadcasted_iota(jnp.int32, (WINDOW, WINDOW), 1)
    older = col > row
    keys = k_ref[:, 0].reshape(-1, SWA_DH)
    values = v_ref[:, 0].reshape(-1, SWA_DH)
    queries = q_ref[:, 0].reshape(-1, SWA_DH)
    old_keys, old_values = halo_ref[0], halo_ref[1]
    seen = older & (chip_ref[0] > 0)
    for b in range(queries.shape[0] // WINDOW):
        rows = slice(b * WINDOW, (b + 1) * WINDOW)
        q, k, v = queries[rows], keys[rows], values[rows]
        old = jnp.where(seen, mat(q, old_keys, NT) * scale, -jnp.inf)
        new = jnp.where(older, -jnp.inf, mat(q, k, NT) * scale)
        peak = jnp.max(jnp.maximum(old, new), axis=-1, keepdims=True)
        old = jnp.exp(old - peak)
        new = jnp.exp(new - peak)
        total = jnp.sum(old + new, axis=-1, keepdims=True)
        old = (old / total).astype(BF)
        new = (new / total).astype(BF)
        out_ref[rows, :] = mat(old, old_values, NN) + mat(new, v, NN)
        old_keys, old_values, seen = k, v, older


def attend(chip, moved, halo):
    rows = moved.shape[2]
    heads = DH // SWA_DH

    def part(i):
        return pl.BlockSpec((2, 1, rows, SWA_DH), lambda h, c: (0, i, 0, h))

    return pl.pallas_call(
        attend_body,
        grid_spec=pltpu.PrefetchScalarGridSpec(
            num_scalar_prefetch=1,
            grid=(heads,),
            in_specs=[
                part(1),
                part(2),
                part(3),
                pl.BlockSpec((2, WINDOW, SWA_DH), lambda h, c: (0, 0, h)),
            ],
            out_specs=pl.BlockSpec((2 * rows, SWA_DH), lambda h, c: (0, h)),
        ),
        out_shape=shape((2 * rows, DH), F32),
        cost_estimate=cost(2 * rows * 8 * WINDOW * DH, 12 * rows * DH, 4 * rows * DH),
        name="window_attention",
    )(chip, moved, moved, moved, halo)


def refresh(weight, update):
    initial = weight.astype(F32)
    stepped = initial - update.astype(F32)
    old_norm = jnp.sqrt(jnp.sum(initial * initial, axis=0, keepdims=True) + epsilon)
    new_norm = jnp.sqrt(jnp.sum(stepped * stepped, axis=0, keepdims=True) + epsilon)
    return (stepped * (old_norm / new_norm)).astype(BF)


def finish_body(core_ref, sum_ref, gate_ref, up_ref, down_ref, q_ref, att_ref, out_ref):
    del core_ref
    iterates = []
    for m in range(3):
        gradient = sum_ref[m].astype(F32)
        norm_total = jnp.sum(gradient * gradient)
        iterates.append((gradient * (1.0 / jnp.sqrt(norm_total + epsilon))).astype(BF))
    for _ in range(NS_ITERS):
        grams = [mat(x, x, NT).astype(BF) for x in iterates]
        polys = [
            (square_coef * g.astype(F32) + quartic_coef * mat(g, g, NN)).astype(BF) for g in grams
        ]
        iterates = [
            (linear_coef * x.astype(F32) + mat(p, x, NN)).astype(BF)
            for p, x in zip(polys, iterates)
        ]
    renewed = [refresh(w[0], x) for w, x in zip((gate_ref, up_ref, down_ref), iterates)]
    queries = q_ref[:, 0].reshape(-1, DH)
    query_gate = mat(queries, renewed[0], NN)
    query_up = mat(queries, renewed[1], NN)
    query_hidden = (query_gate * jax.nn.sigmoid(query_gate) * query_up).astype(BF)
    memory = mat(query_hidden, renewed[2], NN).astype(BF)
    out_ref[...] = (memory.astype(F32) + att_ref[...]).astype(BF)


def finish(core, total, gate, up, down, moved, attended):
    rows = moved.shape[2]
    weight = pl.BlockSpec((1, DH, DH), lambda i, c: (c[0], 0, 0))
    full = pl.BlockSpec((2 * rows, DH), lambda i, c: (0, 0))
    return pl.pallas_call(
        finish_body,
        grid_spec=pltpu.PrefetchScalarGridSpec(
            num_scalar_prefetch=1,
            grid=(1,),
            in_specs=[
                pl.BlockSpec((3, DH, DH), lambda i, c: (0, 0, 0)),
                weight,
                weight,
                weight,
                pl.BlockSpec((2, 1, rows, DH), lambda i, c: (0, 0, 0, 0)),
                full,
            ],
            out_specs=full,
        ),
        out_shape=shape((2 * rows, DH)),
        cost_estimate=cost(42 * DH**3, 20 * DH * DH, rows * DH),
        name="finish",
    )(core, total, gate, up, down, moved, attended)


def unpack_body(in_ref, out_ref):
    out_ref[...] = in_ref[0]


def unpack(moved):
    count, rows, cols = moved.shape
    return pl.pallas_call(
        unpack_body,
        grid=(count,),
        in_specs=[pl.BlockSpec((1, rows, cols), lambda i: (i, 0, 0))],
        out_specs=pl.BlockSpec((rows, cols), lambda i: (0, (i % 2) * 2 + i // 2)),
        out_shape=shape((rows, count * cols)),
        cost_estimate=cost(0, 4 * moved.size),
        name="unpack",
    )(moved)


def swap(value, axes):
    return lax.all_to_all(value, axes, split_axis=0, concat_axis=0, tiled=True)


def shards(fw_q, fw_k, fw_v, fw_lr, fast_gate, fast_up, fast_down, attn_q, attn_k, attn_v):
    core = lax.axis_index("core").astype(jnp.int32).reshape(1)
    chip = lax.axis_index(CHIPS).astype(jnp.int32).reshape(1)
    moved = swap(pack_grad(fw_k, fw_v, fw_lr), "core")
    partial = grads(core, moved, fast_gate, fast_up, fast_down)
    plane = lax.axis_size(PLANE)
    depth = lax.axis_size("z")
    partial, *rest = lax.optimization_barrier((partial, fw_q, attn_q, attn_k, attn_v))
    part = swap(partial.reshape(plane, -1, DH), PLANE)
    moved = swap(pack_rest(rest), "core")
    part = summed(part, 4)
    part, moved = lax.optimization_barrier((part, moved))
    part = swap(part.reshape(depth, -1, DH), "z")
    chips = lax.axis_size(CHIPS)
    halo = lax.ppermute(moved[1, 2:, -WINDOW:], CHIPS, [(s, s + 1) for s in range(chips - 1)])
    part = swap(sum_spread(part), "z").reshape(-1, DH)
    total = swap(spread(part, plane), PLANE).reshape(3, DH, DH)
    attended = attend(chip, moved, halo)
    mixed = finish(core, total, fast_gate, fast_up, fast_down, moved, attended)
    return unpack(swap(mixed.reshape(4, -1, DH), QUAD))


def solution(mesh):
    fine = Mesh(mesh.devices.reshape(8, 4, 2, 2, 2), ("z", "x", "yh", "core", "yl"))
    ctx = ("z", "x", "yh", "core")
    wide = P(ctx, "yl")
    weight = P("yl", None, None)
    in_specs = (wide, wide, wide, wide, weight, weight, weight, wide, wide, wide)
    out_specs = P(ctx + ("yl",), None)
    return jax.shard_map(shards, mesh=fine, in_specs=in_specs, out_specs=out_specs, check_vma=False)
```

time: 171 us -> 157 us (0.918)
  local copies, waits for them, and re-layouts: 43.8 us -> 2.86 us
  Pallas kernels: 0 us -> 38.6 us
  blocking collectives: 11.2 us -> 46.9 us
  matrix products: 33.3 us -> 0 us
  other arithmetic: 12.2 us -> 0 us
  starting transfers between devices: 34.7 us -> 26.2 us
  waiting for transfers between devices: 33.8 us -> 41.2 us
    pallas_call x0 -> x9, Pallas kernels: none -> 38.6 us  [the longest x1 10 us: finish(): pl.pallas_call(finish_body, grid_spec=pltpu.PrefetchScalarGridSpec(num_sc...]
    all_to_all x1 -> x3, blocking collectives: 11.2 us -> 46.9 us  [swap(): return lax.all_to_all(value, axes, split_axis=0, concat_axis=0, tiled=True)]
    dot_general x15 -> x0, matrix products: 33.3 us -> none  [the longest x2 11.8 us: shards(): jnp.einsum('bij,bjk->bik', polynomial, iterate, preferred_element_type=jn...]
    ppermute x1, waiting for transfers between devices: 0.01 us -> 19.8 us  [shards(): lax.ppermute(moved[1, 2:, -WINDOW:], CHIPS, [(s, s + 1) for s in range(ch...]
    unnamed x59 -> x8, local copies, waits for them, and re-layouts: 20.4 us -> 2.84 us
    all_to_all x6 -> x4, waiting for transfers between devices: 33.8 us -> 21.4 us  [swap(): return lax.all_to_all(value, axes, split_axis=0, concat_axis=0, tiled=True)]
    slice x9 -> x0, local copies, waits for them, and re-layouts: 11.1 us -> none  [the longest x4 5.22 us: attend(): window_values = jnp.concatenate([values[:-1], values[1:]], axis=1)]
    all_to_all x6 -> x4, starting transfers between devices: 32.2 us -> 21.4 us  [swap(): return lax.all_to_all(value, axes, split_axis=0, concat_axis=0, tiled=True)]
  transfers between devices with their start and end apart: 7 -> 5, of which waited for: 3 -> 3; matrix products, arithmetic and copies ran while one was open for 32% -> 0% of each run, Pallas kernels for 0% -> 9%
where the time goes in v2:
time: 157 us; the launch traced here: 156 us
  blocking collectives  46.9 us (30%)
  waiting for transfers between devices  41.2 us (26%)
  Pallas kernels  38.6 us (25%)
  starting transfers between devices  26.2 us (17%)
  local copies, waits for them, and re-layouts  2.86 us (2%)
    all_to_all x3, blocking collectives, swap(): return lax.all_to_all(value, axes, split_axis=0, concat_axis=0, tiled=True)  46.9 us
    all_to_all x4, starting transfers between devices, swap(): return lax.all_to_all(value, axes, split_axis=0, concat_axis=0, tiled=True)  21.4 us
    all_to_all x4, waiting for transfers between devices, swap(): return lax.all_to_all(value, axes, split_axis=0, concat_axis=0, tiled=True)  21.4 us
    ppermute x1, waiting for transfers between devices, shards(): lax.ppermute(moved[1, 2:, -WINDOW:], CHIPS, [(s, s + 1) for s in range(ch...  19.8 us
    pallas_call x1, Pallas kernels, finish(): pl.pallas_call(finish_body, grid_spec=pltpu.PrefetchScalarGridSpec(num_sc...  10 us
    pallas_call x1, Pallas kernels, attend(): pl.pallas_call(attend_body, grid_spec=pltpu.PrefetchScalarGridSpec(num_sc...  7.89 us
    pallas_call x1, Pallas kernels, grads(): pl.pallas_call(grads_body, grid_spec=pltpu.PrefetchScalarGridSpec(num_sca...  5.62 us
    ppermute x1, starting transfers between devices, shards(): lax.ppermute(moved[1, 2:, -WINDOW:], CHIPS, [(s, s + 1) for s in range(ch...  4.88 us
  transfers between devices with their start and end apart: 5, of which 3 were waited for; matrix products, arithmetic and copies ran while one was open for 0% of the time, Pallas kernels for 9%

profile of v2, /device:TPU:4, one launch (start us, length us, event | category | flops | bytes accessed | tf_op | source)
XLA Modules:
  0.0 155.8 jit_solution(2164468300143693314)
XLA Ops:
  0.0 2.1 %pack_grad.1 = bf16[2,2,256,512]{3,2,1,0:T(8,128)(2,1)} custom-call(bf16[256,1024]{1,0:T(8,128)(2,1)} %k_ref.1, bf16[256,1024]{1,0:T(8,128)(2,1)} %v_ref.1, f32[2,256]{1,0:T(2,128)} %bitcast.14), custom_call_target="tpu_custom_call" | custom-call | flops 262144 | bytes 2097152 | tf_op jit(solution)/shard_map/pack_grad/pallas_call | solution.py:56
  2.1 3.6 %all-to-all-start = ((bf16[2,2,256,512]{3,2,1,0:T(8,128)(2,1)}), bf16[2,2,256,512]{3,2,1,0:T(8,128)(2,1)S(1)}, u32[]{:S(2)}, u32[]{:S(2)}) async-start(bf16[2,2,256,512]{3,2,1,0:T(8,128)(2,1)} %pack_grad.1), calls=%async_computation | async-start | bytes 2097152 | tf_op jit(solution)/shard_map/all_to_all | solution.py:322
  5.7 2.1 %all-to-all-done.moved_ref = bf16[2,2,256,512]{3,2,1,0:T(8,128)(2,1)S(1)} async-done(((bf16[2,2,256,512]{3,2,1,0:T(8,128)(2,1)}), bf16[2,2,256,512]{3,2,1,0:T(8,128)(2,1)S(1)}, u32[]{:S(2)}, u32[]{:S(2)}) %all-to-all-start) | async-done | bytes 1048608 | tf_op jit(solution)/shard_map/all_to_all | solution.py:322
  7.8 0.0 copy-start.2
  7.8 1.0 copy-done.2
  8.8 5.6 %grads.1 = bf16[3,512,512]{2,1,0:T(8,128)(2,1)} custom-call(s32[1]{0:T(128)} %bitcast.core_ref, bf16[2,2,256,512]{3,2,1,0:T(8,128)(2,1)} %copy-done.2, bf16[2,512,512]{2,1,0:T(8,128)(2,1)} %gate_ref.3, bf16[2,512,512]{2,1,0:T(8,128)(2,1)} %up_ref.3, bf16[2,512,512]{2,1,0:T(8,128)(2,1)} %down_ref.3), custom_call_target="tpu_custom_call" | custom-call | flops 1610612736 | bytes 4194304 | tf_op jit(solution)/shard_map/grads/pallas_call | solution.py:116
  14.4 7.4 %all-to-all-start.1 = ((bf16[8,192,512]{2,1,0:T(8,128)(2,1)}), bf16[8,192,512]{2,1,0:T(8,128)(2,1)S(1)}, u32[]{:S(2)}, u32[]{:S(2)}) async-start(bf16[8,192,512]{2,1,0:T(8,128)(2,1)} %bitcast.10), calls=%async_computation.1 | async-start | bytes 3145728 | tf_op jit(solution)/shard_map/all_to_all | solution.py:322
  21.9 2.6 %pack_rest.1 = bf16[2,4,256,512]{3,2,1,0:T(8,128)(2,1)} custom-call(bf16[256,1024]{1,0:T(8,128)(2,1)} %a_ref, bf16[256,1024]{1,0:T(8,128)(2,1)} %b_ref, bf16[256,1024]{1,0:T(8,128)(2,1)} %c_ref, bf16[256,1024]{1,0:T(8,128)(2,1)} %d_ref), custom_call_target="tpu_custom_call" | custom-call | bytes 4194304 | tf_op jit(solution)/shard_map/pack_rest/pallas_call | solution.py:75
  24.4 19.3 %all-to-all-done.1.in_ref = bf16[8,192,512]{2,1,0:T(8,128)(2,1)S(1)} async-done(((bf16[8,192,512]{2,1,0:T(8,128)(2,1)}), bf16[8,192,512]{2,1,0:T(8,128)(2,1)S(1)}, u32[]{:S(2)}, u32[]{:S(2)}) %all-to-all-start.1) | async-done | bytes 1572896 | tf_op jit(solution)/shard_map/all_to_all | solution.py:322
  43.7 0.0 copy-start.1
  43.7 1.2 copy-done.1
  44.9 3.8 %all-to-all-start.2 = ((bf16[2,4,256,512]{3,2,1,0:T(8,128)(2,1)}), bf16[2,4,256,512]{3,2,1,0:T(8,128)(2,1)S(1)}, u32[]{:S(2)}, u32[]{:S(2)}) async-start(bf16[2,4,256,512]{3,2,1,0:T(8,128)(2,1)} %pack_rest.1), calls=%async_computation.2 | async-start | bytes 4194304 | tf_op jit(solution)/shard_map/all_to_all | solution.py:322
  48.6 3.4 %plane_sum.1 = bf16[192,512]{1,0:T(8,128)(2,1)} custom-call(bf16[8,192,512]{2,1,0:T(8,128)(2,1)} %copy-done.1), custom_call_target="tpu_custom_call" | custom-call | flops 786432 | bytes 1572864 | tf_op jit(solution)/shard_map/plane_sum/pallas_call | solution.py:144
  52.0 0.0 all-to-all-done.2.q_ref.k_ref.v_ref
  52.0 0.0 copy-start
  52.0 19.6 %all_to_all.35.in_ref = bf16[8,24,512]{2,1,0:T(8,128)(2,1)} all-to-all(bf16[8,24,512]{2,1,0:T(8,128)(2,1)} %bitcast.11), channel_id=1, replica_groups=mesh['z'=8,'x'=4,'yh'=2,'core'=2,'yl'=2] {'z'}, dimensions={0} | all-to-all | bytes 393216 | tf_op jit(solution)/shard_map/all_to_all | solution.py:322
  71.7 1.6 %depth_sum.1 = bf16[8,24,512]{2,1,0:T(8,128)(2,1)} custom-call(bf16[8,24,512]{2,1,0:T(8,128)(2,1)} %all_to_all.35.in_ref), custom_call_target="tpu_custom_call" | custom-call | flops 98304 | bytes 393216 | tf_op jit(solution)/shard_map/depth_sum/pallas_call | solution.py:165
  73.3 14.2 %all_to_all.36 = bf16[8,24,512]{2,1,0:T(8,128)(2,1)} all-to-all(bf16[8,24,512]{2,1,0:T(8,128)(2,1)} %depth_sum.1), channel_id=1, replica_groups=mesh['z'=8,'x'=4,'yh'=2,'core'=2,'yl'=2] {'z'}, dimensions={0} | all-to-all | bytes 393216 | tf_op jit(solution)/shard_map/all_to_all | solution.py:322
  87.5 2.2 %spread.1 = bf16[8,192,512]{2,1,0:T(8,128)(2,1)} custom-call(bf16[192,512]{1,0:T(8,128)(2,1)} %bitcast.12), custom_call_target="tpu_custom_call" | custom-call | bytes 1769472 | tf_op jit(solution)/shard_map/spread/pallas_call | solution.py:184
  89.7 6.6 %all-to-all-start.5 = ((bf16[8,192,512]{2,1,0:T(8,128)(2,1)}), bf16[8,192,512]{2,1,0:T(8,128)(2,1)}, u32[]{:S(2)}, u32[]{:S(2)}) async-start(bf16[8,192,512]{2,1,0:T(8,128)(2,1)} %spread.1), calls=%async_computation.5 | async-start | bytes 3145728 | tf_op jit(solution)/shard_map/all_to_all | solution.py:322
  96.2 0.0 copy-done
  96.3 4.9 %collective-permute-start = (bf16[2,128,512]{2,1,0:T(8,128)(2,1)S(1)}, bf16[2,128,512]{2,1,0:T(8,128)(2,1)S(1)}, u32[]{:S(2)}, u32[]{:S(2)}) collective-permute-start(bf16[2,128,512]{2,1,0:T(8,128)(2,1)S(1)} %slice_bitcast_fusion), channel_id=1, source_target_pairs={{0,4},{4,8},{8,12},{12,16},{16,20},{20,24},{24,28},{28,32},{32,36}... | collective-permute-start | bytes 786440 | tf_op jit(solution)/shard_map/ppermute | solution.py:339
  101.2 19.8 %collective-permute-done.halo_ref = bf16[2,128,512]{2,1,0:T(8,128)(2,1)S(1)} collective-permute-done((bf16[2,128,512]{2,1,0:T(8,128)(2,1)S(1)}, bf16[2,128,512]{2,1,0:T(8,128)(2,1)S(1)}, u32[]{:S(2)}, u32[]{:S(2)}) %collective-permute-start) | collective-permute-done | bytes 262176 | tf_op jit(solution)/shard_map/ppermute | solution.py:339
  121.0 0.0 copy-start.3
  121.0 0.7 copy-done.3
  121.7 7.9 %window_attention.1.att_ref = f32[512,512]{1,0:T(8,128)} custom-call(s32[1]{0:T(128)} %bitcast.6.chip_ref, bf16[2,4,256,512]{3,2,1,0:T(8,128)(2,1)} %copy-done, bf16[2,4,256,512]{3,2,1,0:T(8,128)(2,1)} %copy-done, bf16[2,4,256,512]{3,2,1,0:T(8,128)(2,1)} %copy-done, bf16[2,128,512]{2,1,0:T(8,128)(2,1)} %copy-done.3), custom_call_target="tpu_custom_call" | custom-call | flops 268435456 | bytes 1572864 | tf_op jit(solution)/shard_map/window_attention/pallas_call | solution.py:227
  129.6 0.0 all-to-all-done.5
  129.6 10.0 %finish.1 = bf16[512,512]{1,0:T(8,128)(2,1)} custom-call(s32[1]{0:T(128)} %bitcast.core_ref, bf16[3,512,512]{2,1,0:T(8,128)(2,1)} %bitcast.5.sum_ref, bf16[2,512,512]{2,1,0:T(8,128)(2,1)} %gate_ref.3, bf16[2,512,512]{2,1,0:T(8,128)(2,1)} %up_ref.3, bf16[2,512,512]{2,1,0:T(8,128)(2,1)} %down_ref.3, bf16[2,4,256,512]{3,2,1,0:T(8,128)(2,1)} %copy-done, ...), custom_call_target="tpu_custom_call" | custom-call | flops 5637144576 | bytes 5242880 | tf_op jit(solution)/shard_map/finish/pallas_call | solution.py:283
  139.6 13.0 %all_to_all.37.in_ref = bf16[4,128,512]{2,1,0:T(8,128)(2,1)} all-to-all(bf16[4,128,512]{2,1,0:T(8,128)(2,1)} %bitcast.13), channel_id=1, replica_groups=mesh['z'=8,'x'=4,'yh'=2,'core'=2,'yl'=2] {'core','yl'}, dimensions={0} | all-to-all | bytes 1048576 | tf_op jit(solution)/shard_map/all_to_all | solution.py:322
  152.6 3.2 %unpack.1 = bf16[128,2048]{1,0:T(8,128)(2,1)} custom-call(bf16[4,128,512]{2,1,0:T(8,128)(2,1)} %all_to_all.37.in_ref), custom_call_target="tpu_custom_call" | custom-call | bytes 1048576 | tf_op jit(solution)/shard_map/unpack/pallas_call | solution.py:310
  (1 shorter events, 0.0 us)
Async XLA Ops:
  2.1 5.7 %all-to-all-start = ((bf16[2,2,256,512]{3,2,1,0:T(8,128)(2,1)}), bf16[2,2,256,512]{3,2,1,0:T(8,128)(2,1)S(1)}, u32[]{:S(2)}, u32[]{:S(2)}) async-start(bf16[2,2,256,512]{3,2,1,0:T(8,128)(2,1)} %pack_grad.1), calls=%async_computation | async-start | bytes 2097152 | tf_op jit(solution)/shard_map/all_to_all | solution.py:322
  7.8 1.0 copy-start.2
  14.4 29.3 %all-to-all-start.1 = ((bf16[8,192,512]{2,1,0:T(8,128)(2,1)}), bf16[8,192,512]{2,1,0:T(8,128)(2,1)S(1)}, u32[]{:S(2)}, u32[]{:S(2)}) async-start(bf16[8,192,512]{2,1,0:T(8,128)(2,1)} %bitcast.10), calls=%async_computation.1 | async-start | bytes 3145728 | tf_op jit(solution)/shard_map/all_to_all | solution.py:322
  43.7 1.2 copy-start.1
  44.9 7.2 %all-to-all-start.2 = ((bf16[2,4,256,512]{3,2,1,0:T(8,128)(2,1)}), bf16[2,4,256,512]{3,2,1,0:T(8,128)(2,1)S(1)}, u32[]{:S(2)}, u32[]{:S(2)}) async-start(bf16[2,4,256,512]{3,2,1,0:T(8,128)(2,1)} %pack_rest.1), calls=%async_computation.2 | async-start | bytes 4194304 | tf_op jit(solution)/shard_map/all_to_all | solution.py:322
  52.0 44.2 %copy-start = (bf16[2,4,256,512]{3,2,1,0:T(8,128)(2,1)}, bf16[2,4,256,512]{3,2,1,0:T(8,128)(2,1)S(1)}, u32[]{:S(2)}) copy-start(bf16[2,4,256,512]{3,2,1,0:T(8,128)(2,1)S(1)} %all-to-all-done.2.q_ref.k_ref.v_ref) | copy-start | bytes 6291460
  89.7 39.9 %all-to-all-start.5 = ((bf16[8,192,512]{2,1,0:T(8,128)(2,1)}), bf16[8,192,512]{2,1,0:T(8,128)(2,1)}, u32[]{:S(2)}, u32[]{:S(2)}) async-start(bf16[8,192,512]{2,1,0:T(8,128)(2,1)} %spread.1), calls=%async_computation.5 | async-start | bytes 3145728 | tf_op jit(solution)/shard_map/all_to_all | solution.py:322
  96.3 24.7 %collective-permute-start = (bf16[2,128,512]{2,1,0:T(8,128)(2,1)S(1)}, bf16[2,128,512]{2,1,0:T(8,128)(2,1)S(1)}, u32[]{:S(2)}, u32[]{:S(2)}) collective-permute-start(bf16[2,128,512]{2,1,0:T(8,128)(2,1)S(1)} %slice_bitcast_fusion), channel_id=1, source_target_pairs={{0,4},{4,8},{8,12},{12,16},{16,20},{20,24},{24,28},{28,32},{32,36}... | collective-permute-start | bytes 786440 | tf_op jit(solution)/shard_map/ppermute | solution.py:339
  121.0 0.7 copy-start.3
